TPU v7x, 128 devices: a whole 4x4x4 slice. The times are simulated.
128 devices in a mesh: row: 8 (over y, core), col: 16 (over z, x).
Axes of the slice: x: 4, y: 4, z: 4, core: 2. Of those that a mesh axis runs over, the one named last changes fastest.
Arguments:
- hidden_states: bfloat16 [1024, 2048], P('col', 'row'), may hold values from -20 to 20
- input_gain: float32 [2, 2048], P(None, 'row'), may hold values from 0.25 to 1.75
- inner_weight: bfloat16 [2, 2048, 2, 4096], P(None, 'row', None, 'col'), may hold values from -0.125 to 0.125
- proj_weight: bfloat16 [2, 2048, 256], P(None, 'row'), may hold values from -0.125 to 0.125
- step_weight: bfloat16 [2, 2048, 64], P(None, 'row', 'col'), may hold values from -0.125 to 0.125
- inner_kernel: float32 [2, 4, 4096], P(None, None, 'col'), may hold values from -3 to 3
- proj_kernel: float32 [2, 4, 256], replicated, may hold values from -3 to 3
- step_bias: float32 [2, 64], P(None, 'col'), may hold values from -5 to -1
- decay_log: float32 [2, 64], P(None, 'col'), may hold values from -2 to 1
- skip_gain: float32 [2, 64], P(None, 'col'), may hold values from 0.5 to 1.5
- norm_gain: float32 [2, 4096], P(None, 'col'), may hold values from 0.25 to 1.75
- out_weight: bfloat16 [2, 4096, 2048], P(None, 'col', 'row'), may hold values from -0.09375 to 0.09375
- inner_cache: bfloat16 [2, 64, 3, 4096], P(None, 'row', None, 'col'), may hold values from -6 to 6
- proj_cache: bfloat16 [2, 64, 3, 256], P(None, 'row'), may hold values from -6 to 6
- state_cache: float32 [2, 64, 64, 64, 128], P(None, 'row', 'col'), may hold values from -1.2 to 1.2
- accepted: int32 [64], P('row'), may hold values from 1 to 16
- owners: int32 [64], P('row'), may hold values from 0 to 15, as said below
- tenant_ranges: int32 [4, 2], replicated, may hold values from 0 to 64, as said below
Outputs:
- hidden_output: bfloat16 [1024, 2048], P('col', 'row')
- step_states: bfloat16 [2, 64, 16, 64, 64, 128], P(None, 'row', None, 'col')
- owned_states: bfloat16 [8, 16, 2, 2, 64, 64, 128], P('row', 'col')
Inputs may be any that keep to these rules, and one draw needn't show every extreme that they name: `owners`: within the requests of one index of row (aligned blocks of 8) no owner appears more than 2 times, and in every block some owner appears exactly 2 times. `tenant_ranges`: the ranges are in order, disjoint and not empty; exactly 8 requests lie in no range.
All inputs are finite; a program needn't handle non-finite values.
Results may differ from a plain program's by a relative error of at most 0.024.
Values may be sent and summed in bfloat16 or wider, within the bound.
No kernel may reach another device: no remote copies, remote signals or barrier semaphores. Data moves between devices by JAX's collectives and lax.ppermute only.
A program may use at most 128 MiB of HBM per device.

v0:
```python
import jax
import jax.numpy as jnp
from jax import lax
from jax.sharding import PartitionSpec as P

S = 16
SEND_CAP = 2
EPSILON = 1e-05


def conv_silu(prefix, incoming, kernel):
    joined = jnp.concatenate([prefix, incoming], axis=1)
    length = incoming.shape[1]
    summed = joined[:, 0:length, :] * kernel[0]
    for offset in range(1, kernel.shape[0]):
        summed = summed + joined[:, offset : offset + length, :] * kernel[offset]
    return jax.nn.silu(summed)


def ssm_scan(decays, deltas, inner_values, b_values, c_values, skip_values, start_state):

    def advance(carried, packed):
        decay_now, delta_now, value_now, b_now, c_now = packed
        updated = (
            decay_now[:, :, None, None] * carried
            + (delta_now[:, :, None] * value_now)[:, :, :, None] * b_now[:, None, None, :]
        )
        output = (
            jnp.einsum("rhpn,rn->rhp", updated, c_now, precision=lax.Precision.HIGHEST)
            + skip_values[None, :, None] * value_now
        )
        return (updated, (output, updated.astype(jnp.bfloat16)))

    time_major = tuple(
        (
            jnp.moveaxis(member, 1, 0)
            for member in (decays, deltas, inner_values, b_values, c_values)
        )
    )
    last_state, (outputs, states) = lax.scan(advance, start_state, time_major)
    return (jnp.moveaxis(outputs, 0, 1), jnp.moveaxis(states, 0, 1))


def local(
    hidden_states,
    input_gain,
    inner_weight,
    proj_weight,
    step_weight,
    inner_kernel,
    proj_kernel,
    step_bias,
    decay_log,
    skip_gain,
    norm_gain,
    out_weight,
    inner_cache,
    proj_cache,
    state_cache,
    accepted,
    owners,
    tenant_ranges,
):
    layer_count = inner_weight.shape[0]
    row_width = inner_weight.shape[1]
    inner_local = inner_weight.shape[3]
    heads_local = step_weight.shape[2]
    head_size = inner_local // heads_local
    state_size = proj_weight.shape[2] // 2
    requests_local = state_cache.shape[1]
    draft_steps = S
    row_count = lax.axis_size("row")
    col_count = lax.axis_size("col")
    model_width = row_width * row_count
    inner_width = inner_local * col_count
    token_rows = requests_local * draft_steps
    local_ids = jnp.arange(requests_local, dtype=jnp.int32)
    request_ids = lax.axis_index("row") * requests_local + local_ids
    live_mask = jnp.any(
        (request_ids[:, None] >= tenant_ranges[None, :, 0])
        & (request_ids[:, None] < tenant_ranges[None, :, 1]),
        axis=1,
    )
    earlier = (owners[:, None] == owners[None, :]) & (local_ids[None, :] < local_ids[:, None])
    slot_ranks = jnp.sum(earlier.astype(jnp.int32), axis=1)
    slot_ids = owners * SEND_CAP + slot_ranks
    slot_grid = jnp.arange(col_count * SEND_CAP, dtype=jnp.int32)
    step_grid = jnp.arange(draft_steps, dtype=jnp.int32)
    picker = (
        (slot_grid[:, None, None] == slot_ids[None, :, None])
        & (step_grid[None, None, :] == accepted[None, :, None] - 1)
        & live_mask[None, :, None]
    )
    picker = picker.astype(jnp.bfloat16).reshape(col_count * SEND_CAP, token_rows)
    hidden = hidden_states
    step_outputs = []
    chosen_layers = []
    for layer_index in range(layer_count):
        all_tokens = lax.all_gather(hidden, "col", axis=0, tiled=True)
        tokens_f = all_tokens.astype(jnp.float32)
        scaled = (tokens_f * input_gain[layer_index]).astype(jnp.bfloat16)
        square_part = jnp.sum(tokens_f * tokens_f, axis=1)
        inner_part = jnp.dot(
            scaled,
            inner_weight[layer_index].reshape(row_width, 2 * inner_local),
            preferred_element_type=jnp.float32,
        )
        step_part = jnp.dot(scaled, step_weight[layer_index], preferred_element_type=jnp.float32)
        proj_part = jnp.dot(scaled, proj_weight[layer_index], preferred_element_type=jnp.float32)
        inner_sum, step_sum, proj_sum, square_sum = (
            lax.psum_scatter(inner_part, "row", scatter_dimension=0, tiled=True),
            lax.psum_scatter(step_part, "row", scatter_dimension=0, tiled=True),
            lax.psum_scatter(proj_part, "row", scatter_dimension=0, tiled=True),
            lax.psum_scatter(square_part, "row", scatter_dimension=0, tiled=True),
        )
        inverse_rms = lax.rsqrt(square_sum / model_width + EPSILON)
        inner_vals = inner_sum * inverse_rms[:, None]
        gate_vals = inner_vals[:, :inner_local]
        raw_inner = inner_vals[:, inner_local:].reshape(requests_local, draft_steps, inner_local)
        raw_proj = (proj_sum * inverse_rms[:, None]).reshape(
            requests_local, draft_steps, 2 * state_size
        )
        conv_inner = conv_silu(
            inner_cache[layer_index].astype(jnp.float32), raw_inner, inner_kernel[layer_index]
        )
        conv_proj = conv_silu(
            proj_cache[layer_index].astype(jnp.float32), raw_proj, proj_kernel[layer_index]
        )
        deltas = jax.nn.softplus(
            (step_sum * inverse_rms[:, None]).reshape(requests_local, draft_steps, heads_local)
            + step_bias[layer_index]
        )
        decays = jnp.exp(-deltas * jnp.exp(decay_log[layer_index]))
        outputs, states = ssm_scan(
            decays,
            deltas,
            conv_inner.reshape(requests_local, draft_steps, heads_local, head_size),
            conv_proj[..., :state_size],
            conv_proj[..., state_size:],
            skip_gain[layer_index],
            state_cache[layer_index],
        )
        step_outputs.append(states)
        gated_raw = outputs.reshape(token_rows, inner_local) * jax.nn.silu(gate_vals)
        gate_square = lax.psum(jnp.sum(gated_raw * gated_raw, axis=1), "col")
        gated = (
            gated_raw
            * norm_gain[layer_index]
            * lax.rsqrt(gate_square / inner_width + EPSILON)[:, None]
        ).astype(jnp.bfloat16)
        layer_weight = out_weight[layer_index]
        partial_out = jnp.dot(
            lax.all_gather(gated, "row", axis=0, tiled=True),
            layer_weight,
            preferred_element_type=jnp.float32,
        )
        out_sum = lax.psum_scatter(
            partial_out.astype(jnp.bfloat16), "col", scatter_dimension=0, tiled=True
        ).astype(jnp.float32)
        hidden = (hidden.astype(jnp.float32) + out_sum).astype(jnp.bfloat16)
        chosen = jnp.dot(
            picker,
            states.reshape(token_rows, heads_local * head_size * state_size),
            preferred_element_type=jnp.float32,
        )
        chosen = chosen.astype(jnp.bfloat16).reshape(
            col_count, SEND_CAP, heads_local, head_size, state_size
        )
        chosen_layers.append(chosen)
    gathered = lax.all_to_all(
        jnp.stack(chosen_layers, axis=2), "col", split_axis=0, concat_axis=3, tiled=True
    )
    owned_block = gathered[None]
    step_all = jnp.stack(step_outputs, axis=0)
    return (hidden, step_all, owned_block)


def solution(mesh):
    placed = (
        P("col", "row"),
        P(None, "row"),
        P(None, "row", None, "col"),
        P(None, "row", None),
        P(None, "row", "col"),
        P(None, None, "col"),
        P(),
        P(None, "col"),
        P(None, "col"),
        P(None, "col"),
        P(None, "col"),
        P(None, "col", "row"),
        P(None, "row", None, "col"),
        P(None, "row", None, None),
        P(None, "row", "col", None, None),
        P("row"),
        P("row"),
        P(),
    )
    return jax.shard_map(
        local,
        mesh=mesh,
        in_specs=placed,
        out_specs=(
            P("col", "row"),
            P(None, "row", None, "col", None, None),
            P("row", "col", None, None, None, None, None),
        ),
        check_vma=False,
    )
```

profile of v0, /device:TPU:0, one launch (start us, length us, event | category | flops | bytes accessed | tf_op | source)
XLA Modules:
  0.0 788.9 jit_solution(10721165272953729870)
XLA Ops:
  8.6 25.4 %all_gather.12 = bf16[1024,256]{1,0:T(8,128)(2,1)S(1)} all-gather(bf16[64,256]{1,0:T(8,128)(2,1)} %param.22), channel_id=1, replica_groups=mesh['row'=8,'col'=16] {'col'}, dimensions={0}, use_global_device_ids=true | all-gather | bytes 557056 | tf_op jit(solution)/shard_map/all_gather | solution.py:99
  42.9 12.5 %all-reduce = f32[1024]{0:T(1024)S(1)} all-reduce(f32[1024]{0:T(1024)S(1)} %fusion.5), channel_id=3, replica_groups=mesh['row'=8,'col'=16] {'row'}, use_global_device_ids=true, to_apply=%region_2.0.clone | all-reduce | flops 1024 | bytes 8192
  60.8 5.6 reduce-scatter.25.cloned.1.call-done
  69.0 31.3 %reduce-scatter.15.cloned.1.call-done = f32[128,256]{1,0:T(8,128)} async-done(((f32[1024,256]{1,0:T(8,128)}), f32[128,256]{1,0:T(8,128)}) %reduce-scatter.15.cloned.1.call-update) | async-done | bytes 131088 | tf_op jit(solution)/shard_map/reduce_scatter | solution.py:113
  102.1 33.8 %reduce-scatter.13.cloned.1.call-done = f32[128,512]{1,0:T(8,128)} async-done(((f32[1024,512]{1,0:T(8,128)}), f32[128,512]{1,0:T(8,128)}) %reduce-scatter.13.cloned.1.call-update) | async-done | bytes 262160 | tf_op jit(solution)/shard_map/reduce_scatter | solution.py:111
  137.4 5.4 broadcast.153.clone2
  142.7 103.3 %while.28 = (s32[]{:T(128)}, f32[8,4,64,128]{3,2,1,0:T(8,128)S(1)}, f32[16,8,4,64]{3,2,1,0:T(4,128)S(1)}, bf16[16,8,4,64,128]{4,3,2,0,1:T(8,128)(2,1)}, f32[16,8...) while((s32[]{:T(128)}, f32[8,4,64,128]{3,2,1,0:T(8,128)S(1)}, ...), condition=%wide.region_6.0_spmd, body=%wide.region_5.0_spmd.sunk | while | flops 4200450 | bytes 3777949 | solution.py:40
  145.9 2.5 fusion.99
  158.8 2.5 fusion.99
  165.3 2.5 fusion.99
  171.7 2.5 fusion.99
  178.2 2.5 fusion.99
  184.6 2.5 fusion.99
  246.5 40.5 %psum.14 = f32[128]{0:T(128)S(1)} all-reduce(f32[128]{0:T(128)S(1)} %get-tuple-element.179), channel_id=1, replica_groups=mesh['row'=8,'col'=16] {'col'}, use_global_device_ids=true, to_apply=%region_8.9 | all-reduce | flops 128 | bytes 1024 | tf_op jit(solution)/shard_map/psum | solution.py:145
  287.8 13.1 %all_gather.13 = bf16[1024,256]{1,0:T(8,128)(2,1)S(1)} all-gather(bf16[128,256]{1,0:T(8,128)(2,1)S(1)} %multiply_convert_fusion.1), channel_id=1, replica_groups=mesh['row'=8,'col'=16] {'row'}, dimensions={0}, use_global_device_ids=true | all-gather | bytes 589824 | tf_op jit(solution)/shard_map/all_gather | solution.py:153
  302.9 67.3 %reduce-scatter.17.cloned.1.call-done = bf16[64,256]{1,0:T(8,128)(2,1)} async-done(((bf16[1024,256]{1,0:T(8,128)(2,1)}), bf16[64,256]{1,0:T(8,128)(2,1)}) %reduce-scatter.17.cloned.1.call-update) | async-done | bytes 32784 | tf_op jit(solution)/shard_map/reduce_scatter | solution.py:157
  371.0 23.3 %all_gather.14 = bf16[1024,256]{1,0:T(8,128)(2,1)S(1)} all-gather(bf16[64,256]{1,0:T(8,128)(2,1)S(1)} %add_convert_fusion.1), channel_id=1, replica_groups=mesh['row'=8,'col'=16] {'col'}, dimensions={0}, use_global_device_ids=true | all-gather | bytes 557056 | tf_op jit(solution)/shard_map/all_gather | solution.py:99
  400.6 13.3 %reshape.291 = bf16[128,32768]{1,0:T(8,128)(2,1)} reshape(bf16[8,16,4,64,128]{4,3,2,1,0:T(8,128)(2,1)} %bitcast.249) | data formatting | bytes 16777216 | tf_op jit(solution)/shard_map/reshape | solution.py:163
  414.0 4.7 fusion.2
  420.7 12.6 %all-reduce.1 = f32[1024]{0:T(1024)S(1)} all-reduce(f32[1024]{0:T(1024)S(1)} %fusion.7), channel_id=8, replica_groups=mesh['row'=8,'col'=16] {'row'}, use_global_device_ids=true, to_apply=%region_12.13.clone | all-reduce | flops 1024 | bytes 8192
  434.7 24.2 %reduce-scatter.21.cloned.1.call-done = f32[128,256]{1,0:T(8,128)} async-done(((f32[1024,256]{1,0:T(8,128)}), f32[128,256]{1,0:T(8,128)}) %reduce-scatter.21.cloned.1.call-update) | async-done | bytes 131088 | tf_op jit(solution)/shard_map/reduce_scatter | solution.py:113
  460.1 34.4 %reduce-scatter.19.cloned.1.call-done = f32[128,512]{1,0:T(8,128)} async-done(((f32[1024,512]{1,0:T(8,128)}), f32[128,512]{1,0:T(8,128)}) %reduce-scatter.19.cloned.1.call-update) | async-done | bytes 262160 | tf_op jit(solution)/shard_map/reduce_scatter | solution.py:111
  496.0 5.4 broadcast.153.clone
  501.4 70.9 %while.29 = (s32[]{:T(128)}, f32[8,4,64,128]{3,2,1,0:T(8,128)S(1)}, f32[16,8,4,64]{3,2,1,0:T(4,128)S(1)}, bf16[16,8,4,64,128]{4,3,2,0,1:T(8,128)(2,1)}, f32[16,8...) while((s32[]{:T(128)}, f32[8,4,64,128]{3,2,1,0:T(8,128)S(1)}, ...), condition=%wide.region_16.17_spmd, body=%wide.region_15.16_spmd.sunk | while | flops 4200450 | bytes 3778445 | solution.py:40
  572.4 13.3 %reshape.292 = bf16[128,32768]{1,0:T(8,128)(2,1)} reshape(bf16[8,16,4,64,128]{4,3,2,1,0:T(8,128)(2,1)} %bitcast.247) | data formatting | bytes 16777216 | tf_op jit(solution)/shard_map/reshape | solution.py:163
  585.6 4.8 fusion.3
  593.3 7.0 all-to-all-start
  600.8 81.9 %psum.15 = f32[128]{0:T(128)S(1)} all-reduce(f32[128]{0:T(128)S(1)} %get-tuple-element.177), channel_id=1, replica_groups=mesh['row'=8,'col'=16] {'col'}, use_global_device_ids=true, to_apply=%region_18.19 | all-reduce | flops 128 | bytes 1024 | tf_op jit(solution)/shard_map/psum | solution.py:145
  682.8 21.8 %all_gather.15 = bf16[1024,256]{1,0:T(8,128)(2,1)S(1)} all-gather(bf16[128,256]{1,0:T(8,128)(2,1)S(1)} %multiply_convert_fusion), channel_id=1, replica_groups=mesh['row'=8,'col'=16] {'row'}, dimensions={0}, use_global_device_ids=true | all-gather | bytes 589824 | tf_op jit(solution)/shard_map/all_gather | solution.py:153
  705.7 13.8 %pad_maximum_fusion = bf16[2,8,16,4,64,128]{5,4,3,2,1,0:T(8,128)(2,1)} fusion(bf16[1,8,16,4,64,128]{5,4,3,2,1,0:T(8,128)(2,1)} %bitcast.248, bf16[1,8,16,4,64,128]{5,4,3,2,1,0:T(8,128)(2,1)} %bitcast.250), kind=kLoop, calls=%fused_computation.22 | loop fusion | flops 8388608 | bytes 33554432 | tf_op jit(solution)/shard_map/stack | solution.py:174
  719.5 55.1 %reduce-scatter.23.cloned.1.call-done = bf16[64,256]{1,0:T(8,128)(2,1)} async-done(((bf16[1024,256]{1,0:T(8,128)(2,1)}), bf16[64,256]{1,0:T(8,128)(2,1)}) %reduce-scatter.23.cloned.1.call-update) | async-done | bytes 32784 | tf_op jit(solution)/shard_map/reduce_scatter | solution.py:157
  776.1 6.0 copy.143
  (439 shorter events, 201.0 us)
Async XLA Ops:
  7.2 48.3 %copy-start.22 = (f32[2,4]{1,0:T(2,128)S(1)}, f32[2,4]{1,0:T(2,128)}, u32[]{:S(2)}) copy-start(f32[2,4]{1,0:T(2,128)} %param.31) | copy-start | bytes 100
  7.2 48.9 %copy-start.21 = (f32[2,256]{1,0:T(2,128)S(1)}, f32[2,256]{1,0:T(2,128)}, u32[]{:S(2)}) copy-start(f32[2,256]{1,0:T(2,128)} %param.32) | copy-start | bytes 6148
  7.2 49.5 %copy-start.25 = (f32[2,4]{1,0:T(2,128)S(1)}, f32[2,4]{1,0:T(2,128)}, u32[]{:S(2)}) copy-start(f32[2,4]{1,0:T(2,128)} %param.30) | copy-start | bytes 100
  7.2 49.5 %copy-start.24 = (f32[2,4]{1,0:T(2,128)S(1)}, f32[2,4]{1,0:T(2,128)}, u32[]{:S(2)}) copy-start(f32[2,4]{1,0:T(2,128)} %param.29) | copy-start | bytes 100
  7.2 50.0 %copy-start.8 = (f32[2,4,256]{2,1,0:T(4,128)S(1)}, f32[2,4,256]{2,1,0:T(4,128)}, u32[]{:S(2)}) copy-start(f32[2,4,256]{2,1,0:T(4,128)} %param.27) | copy-start | bytes 24580
  7.2 50.6 %copy-start.9 = (f32[2,4,256]{2,1,0:T(4,128)S(1)}, f32[2,4,256]{2,1,0:T(4,128)}, u32[]{:S(2)}) copy-start(f32[2,4,256]{2,1,0:T(4,128)} %param.28) | copy-start | bytes 24580
  7.2 51.2 %copy-start.5 = (bf16[2,8,3,256]{3,1,2,0:T(8,128)(2,1)S(1)}, bf16[2,8,3,256]{3,1,2,0:T(8,128)(2,1)}, u32[]{:S(2)}) copy-start(bf16[2,8,3,256]{3,1,2,0:T(8,128)(2,1)} %param.34) | copy-start | bytes 73732
  7.3 51.2 %copy-start.6 = (bf16[2,8,3,256]{3,1,2,0:T(8,128)(2,1)S(1)}, bf16[2,8,3,256]{3,1,2,0:T(8,128)(2,1)}, u32[]{:S(2)}) copy-start(bf16[2,8,3,256]{3,1,2,0:T(8,128)(2,1)} %param.35) | copy-start | bytes 73732
  7.3 59.2 %reduce-scatter.25.cloned.1.call-start = ((), (), s32[]{:S(2)}) async-start(), calls=%async_computation.15 | async-start | bytes 589824
  35.9 64.4 %reduce-scatter.15.cloned.1.call-start = ((), (), s32[]{:S(2)}) async-start(), calls=%async_computation.10 | async-start | bytes 1179648 | tf_op jit(solution)/shard_map/reduce_scatter | solution.py:113
  38.1 97.8 %reduce-scatter.13.cloned.1.call-start = ((), (), s32[]{:S(2)}) async-start(), calls=%async_computation.9 | async-start | bytes 2359296 | tf_op jit(solution)/shard_map/reduce_scatter | solution.py:111
  41.4 328.8 %reduce-scatter.17.cloned.1.call-start = ((), (), s32[]{:S(2)}) async-start(), calls=%async_computation.11 | async-start | bytes 557056 | tf_op jit(solution)/shard_map/reduce_scatter | solution.py:157
  142.7 227.5 %copy-start.3 = (bf16[64,256]{1,0:T(8,128)(2,1)S(1)}, bf16[64,256]{1,0:T(8,128)(2,1)}, u32[]{:S(2)}) copy-start(bf16[64,256]{1,0:T(8,128)(2,1)} %param.22) | copy-start | bytes 98308
  142.7 253.4 %copy-start.1 = (bf16[2,256,256]{2,1,0:T(8,128)(2,1)S(1)}, bf16[2,256,256]{2,1,0:T(8,128)(2,1)}, u32[]{:S(2)}) copy-start(bf16[2,256,256]{2,1,0:T(8,128)(2,1)} %param.25) | copy-start | bytes 786436
  246.1 152.2 %copy-start.7 = (f32[1,256]{1,0:T(1,128)S(1)}, f32[1,256]{1,0:T(1,128)}, u32[]{:S(2)}) copy-start(f32[1,256]{1,0:T(1,128)} %get-tuple-element.219) | copy-start | bytes 3076
  246.1 154.0 %copy-start.27 = (s32[8]{0:T(128)S(1)}, s32[8]{0:T(128)}, u32[]{:S(2)}) copy-start(s32[8]{0:T(128)} %param.38) | copy-start | bytes 100
  246.1 154.2 %copy-start.23 = (s32[4,2]{0,1:T(2,128)S(1)}, s32[4,2]{0,1:T(2,128)}, u32[]{:S(2)}) copy-start(s32[4,2]{0,1:T(2,128)} %param.39) | copy-start | bytes 100
  246.1 154.3 %copy-start.26 = (s32[8]{0:T(128)S(1)}, s32[8]{0:T(128)}, u32[]{:S(2)}) copy-start(s32[8]{0:T(128)} %param.37) | copy-start | bytes 100
  302.9 130.5 %reduce-scatter.27.cloned.1.call-start = ((), (), s32[]{:S(2)}) async-start(), calls=%async_computation.16 | async-start | bytes 589824
  396.1 62.8 %reduce-scatter.21.cloned.1.call-start = ((), (), s32[]{:S(2)}) async-start(), calls=%async_computation.13 | async-start | bytes 1179648 | tf_op jit(solution)/shard_map/reduce_scatter | solution.py:113
  398.2 96.4 %reduce-scatter.19.cloned.1.call-start = ((), (), s32[]{:S(2)}) async-start(), calls=%async_computation.12 | async-start | bytes 2359296 | tf_op jit(solution)/shard_map/reduce_scatter | solution.py:111
  413.9 46.1 %copy-start.15 = (f32[1,1,256]{2,1,0:T(1,128)S(1)}, f32[1,1,256]{2,1,0:T(1,128)}, u32[]{:S(2)}) copy-start(f32[1,1,256]{2,1,0:T(1,128)} %get-tuple-element.202) | copy-start | bytes 3076
  413.9 46.1 %copy-start.16 = (f32[1,1,256]{2,1,0:T(1,128)S(1)}, f32[1,1,256]{2,1,0:T(1,128)}, u32[]{:S(2)}) copy-start(f32[1,1,256]{2,1,0:T(1,128)} %get-tuple-element.207) | copy-start | bytes 3076
  413.9 46.1 %copy-start.17 = (f32[1,1,256]{2,1,0:T(1,128)S(1)}, f32[1,1,256]{2,1,0:T(1,128)}, u32[]{:S(2)}) copy-start(f32[1,1,256]{2,1,0:T(1,128)} %get-tuple-element.208) | copy-start | bytes 3076
  414.0 81.8 %copy-start.10 = (f32[1,1,256]{2,1,0:T(1,128)S(1)}, f32[1,1,256]{2,1,0:T(1,128)}, u32[]{:S(2)}) copy-start(f32[1,1,256]{2,1,0:T(1,128)} %get-tuple-element.209) | copy-start | bytes 3076
  414.0 81.8 %copy-start.11 = (f32[1,1,256]{2,1,0:T(1,128)S(1)}, f32[1,1,256]{2,1,0:T(1,128)}, u32[]{:S(2)}) copy-start(f32[1,1,256]{2,1,0:T(1,128)} %get-tuple-element.210) | copy-start | bytes 3076
  414.0 81.8 %copy-start.12 = (f32[1,1,256]{2,1,0:T(1,128)S(1)}, f32[1,1,256]{2,1,0:T(1,128)}, u32[]{:S(2)}) copy-start(f32[1,1,256]{2,1,0:T(1,128)} %get-tuple-element.215) | copy-start | bytes 3076
  414.0 81.8 %copy-start.13 = (f32[1,1,256]{2,1,0:T(1,128)S(1)}, f32[1,1,256]{2,1,0:T(1,128)}, u32[]{:S(2)}) copy-start(f32[1,1,256]{2,1,0:T(1,128)} %get-tuple-element.216) | copy-start | bytes 3076
  590.9 91.8 %copy-start.18 = (f32[1,256]{1,0:T(1,128)S(1)}, f32[1,256]{1,0:T(1,128)}, u32[]{:S(2)}) copy-start(f32[1,256]{1,0:T(1,128)} %get-tuple-element.217) | copy-start | bytes 3076
  590.9 113.7 %copy-start.2 = (bf16[2,256,256]{2,1,0:T(8,128)(2,1)S(1)}, bf16[2,256,256]{2,1,0:T(8,128)(2,1)}, u32[]{:S(2)}) copy-start(bf16[2,256,256]{2,1,0:T(8,128)(2,1)} %param.33) | copy-start | bytes 786436
  593.3 182.7 %all-to-all-start = ((bf16[16,2,2,4,64,128]{5,4,3,1,2,0:T(8,128)(2,1)}), bf16[16,2,2,4,64,128]{5,4,3,1,2,0:T(8,128)(2,1)}, u32[]{:S(2)}, u32[]{:S(2)}) async-start(bf16[16,2,2,4,64,128]{5,4,3,1,2,0:T(8,128)(2,1)} %pad_maximum_fusion.1), calls=%async_computation.6 | async-start | bytes 8388608 | tf_op jit(solution)/shard_map/all_to_all | solution.py:170
  600.3 174.4 %reduce-scatter.23.cloned.1.call-start = ((), (), s32[]{:S(2)}) async-start(), calls=%async_computation.14 | async-start | bytes 557056 | tf_op jit(solution)/shard_map/reduce_scatter | solution.py:157
  (6 other events, 172.7 us)
Sparse Core Ops, SparseCore 0:
  36.0 30.4 reduce-scatter.24
  69.5 30.7 reduce-scatter.14
  103.4 32.4 reduce-scatter.12
  303.0 67.1 reduce-scatter.16
  396.2 29.5 reduce-scatter.26
  428.2 30.6 reduce-scatter.20
  462.0 32.5 reduce-scatter.18
  705.8 68.7 reduce-scatter.22
where the time goes:
time: 792 us; the launch traced here: 789 us
  waiting for transfers between devices  252 us (32%)
  blocking collectives  231 us (29%)
  matrix products  105 us (13%)
  other arithmetic  90.8 us (11%)
  local copies, waits for them, and re-layouts  86.9 us (11%)
  between operations  15.4 us (2%)
    psum x2, blocking collectives, local(): gate_square = lax.psum(jnp.sum(gated_raw * gated_raw, axis=1), 'col')  122 us
    reduce_scatter x2, waiting for transfers between devices, local(): lax.psum_scatter(partial_out.astype(jnp.bfloat16), 'col', scatter_dimensi...  122 us
    dot_general x32, matrix products, advance(): jnp.einsum('rhpn,rn->rhp', updated, c_now, precision=lax.Precision.HIGHEST)  80.9 us
    reduce_scatter x2, waiting for transfers between devices, local(): lax.psum_scatter(inner_part, 'row', scatter_dimension=0, tiled=True)  68.3 us
    dynamic_update_slice x64, other arithmetic, ssm_scan(): last_state, (outputs, states) = lax.scan(advance, start_state, time_major)  62.7 us
    reduce_scatter x2, waiting for transfers between devices, local(): lax.psum_scatter(proj_part, 'row', scatter_dimension=0, tiled=True)  55.6 us
    all_gather x2, blocking collectives, local(): all_tokens = lax.all_gather(hidden, 'col', axis=0, tiled=True)  48.8 us
    all_gather x2, blocking collectives, local(): lax.all_gather(gated, 'row', axis=0, tiled=True)  34.9 us
  transfers between devices with their start and end apart: 9, of which 7 were waited for; matrix products, arithmetic and copies ran while one was open for 8% of the time, Pallas kernels for 0%

commit v1 on v0

--- a/solution.py
+++ b/solution.py
@@ -96,7 +96,14 @@
     step_outputs = []
     chosen_layers = []
     for layer_index in range(layer_count):
-        all_tokens = lax.all_gather(hidden, "col", axis=0, tiled=True)
+        ring = [hidden]
+        for hop in range(15):
+            ring.append(lax.ppermute(ring[-1], "col", [(dev, (dev + 1) % 16) for dev in range(16)]))
+        all_tokens = jnp.roll(
+            jnp.concatenate(ring[::-1], axis=0),
+            (lax.axis_index("col") + 1) * ring[0].shape[0],
+            axis=0,
+        )
         tokens_f = all_tokens.astype(jnp.float32)
         scaled = (tokens_f * input_gain[layer_index]).astype(jnp.bfloat16)
         square_part = jnp.sum(tokens_f * tokens_f, axis=1)

time: 792 us -> 1020 us (1.29)
  waiting for transfers between devices: 252 us -> 462 us
  blocking collectives: 231 us -> 182 us
  local copies, waits for them, and re-layouts: 86.9 us -> 122 us
  other arithmetic: 90.8 us -> 114 us
    ppermute x0 -> x30, waiting for transfers between devices: none -> 215 us  [local(): lax.ppermute(ring[-1], 'col', [(dev, (dev + 1) % 16) for dev in range(16)])]
    all_gather x2 -> x0, blocking collectives: 48.8 us -> none  [local(): all_tokens = lax.all_gather(hidden, 'col', axis=0, tiled=True)]
    mul x32, other arithmetic: 2.37 us -> 13.8 us  [advance(): delta_now[:, :, None] * value_now]
    dynamic_slice x32, local copies, waits for them, and re-layouts: 0.05 us -> 11 us  [ssm_scan(): last_state, (outputs, states) = lax.scan(advance, start_state, time_major)]
    mul x64, local copies, waits for them, and re-layouts: 13.8 us -> 24.7 us  [advance(): delta_now[:, :, None] * value_now]
    mul x32, local copies, waits for them, and re-layouts: 11.3 us -> 22 us  [advance(): (delta_now[:, :, None] * value_now)[:, :, :, None] * b_now[:, None, None, :]]
  transfers between devices with their start and end apart: 9 -> 39, of which waited for: 7 -> 37; matrix products, arithmetic and copies ran while one was open for 8% -> 6% of each run, Pallas kernels for 0% -> 0%
where the time goes in v1:
time: 1020 us; the launch traced here: 1010 us
  waiting for transfers between devices  462 us (45%)
  blocking collectives  182 us (18%)
  local copies, waits for them, and re-layouts  122 us (12%)
  other arithmetic  114 us (11%)
  matrix products  103 us (10%)
  between operations  15.6 us (2%)
    ppermute x30, waiting for transfers between devices, local(): lax.ppermute(ring[-1], 'col', [(dev, (dev + 1) % 16) for dev in range(16)])  215 us
    psum x2, blocking collectives, local(): gate_square = lax.psum(jnp.sum(gated_raw * gated_raw, axis=1), 'col')  123 us
    reduce_scatter x2, waiting for transfers between devices, local(): lax.psum_scatter(partial_out.astype(jnp.bfloat16), 'col', scatter_dimensi...  122 us
    dot_general x32, matrix products, advance(): jnp.einsum('rhpn,rn->rhp', updated, c_now, precision=lax.Precision.HIGHEST)  80.9 us
    dynamic_update_slice x64, other arithmetic, ssm_scan(): last_state, (outputs, states) = lax.scan(advance, start_state, time_major)  72.6 us
    reduce_scatter x2, waiting for transfers between devices, local(): lax.psum_scatter(inner_part, 'row', scatter_dimension=0, tiled=True)  67.6 us
    reduce_scatter x2, waiting for transfers between devices, local(): lax.psum_scatter(proj_part, 'row', scatter_dimension=0, tiled=True)  54.4 us
    all_gather x2, blocking collectives, local(): lax.all_gather(gated, 'row', axis=0, tiled=True)  34.6 us
  transfers between devices with their start and end apart: 39, of which 37 were waited for; matrix products, arithmetic and copies ran while one was open for 6% of the time, Pallas kernels for 0%

profile of v1, /device:TPU:0, one launch (start us, length us, event | category | flops | bytes accessed | tf_op | source)
XLA Modules:
  0.0 1009.4 jit_solution(4031153861265545026)
XLA Ops:
  15.8 7.2 collective-permute-done.1
  23.0 7.2 collective-permute-done.2
  30.3 7.2 collective-permute-done.3
  37.5 7.2 collective-permute-done.4
  44.7 7.2 collective-permute-done.5
  52.0 7.2 collective-permute-done.6
  59.2 7.2 collective-permute-done.7
  66.4 7.2 collective-permute-done.8
  73.7 7.2 collective-permute-done.9
  80.9 7.4 collective-permute-done.10
  88.3 7.2 collective-permute-done.11
  95.6 7.2 collective-permute-done.12
  102.8 7.2 collective-permute-done.13
  133.6 12.6 %all-reduce = f32[1024]{0:T(1024)S(1)} all-reduce(f32[1024]{0:T(1024)S(1)} %get-tuple-element.184), channel_id=3, replica_groups=mesh['row'=8,'col'=16] {'row'}, use_global_device_ids=true, to_apply=%region_2.4.clone | all-reduce | flops 1024 | bytes 8192
  150.9 31.3 %reduce-scatter.15.cloned.1.call-done = f32[128,256]{1,0:T(8,128)} async-done(((f32[1024,256]{1,0:T(8,128)}), f32[128,256]{1,0:T(8,128)}) %reduce-scatter.15.cloned.1.call-update) | async-done | bytes 131088 | tf_op jit(solution)/shard_map/reduce_scatter | solution.py:120
  184.1 33.9 %reduce-scatter.13.cloned.1.call-done = f32[128,512]{1,0:T(8,128)} async-done(((f32[1024,512]{1,0:T(8,128)}), f32[128,512]{1,0:T(8,128)}) %reduce-scatter.13.cloned.1.call-update) | async-done | bytes 262160 | tf_op jit(solution)/shard_map/reduce_scatter | solution.py:118
  224.8 92.4 %while.28 = (s32[]{:T(128)}, f32[8,4,64,128]{3,2,1,0:T(8,128)S(1)}, f32[16,8,4,64]{3,2,1,0:T(4,128)S(1)}, bf16[16,8,4,64,128]{4,3,2,0,1:T(8,128)(2,1)}, f32[16,8...) while((s32[]{:T(128)}, f32[8,4,64,128]{3,2,1,0:T(8,128)S(1)}, ...), condition=%wide.region_6.8_spmd, body=%wide.region_5.7_spmd.sunk | while | flops 4200450 | bytes 3778445 | solution.py:40
  317.6 40.5 %psum.14 = f32[128]{0:T(128)S(1)} all-reduce(f32[128]{0:T(128)S(1)} %get-tuple-element.182), channel_id=1, replica_groups=mesh['row'=8,'col'=16] {'col'}, use_global_device_ids=true, to_apply=%region_8.10 | all-reduce | flops 128 | bytes 1024 | tf_op jit(solution)/shard_map/psum | solution.py:152
  358.3 13.1 %all_gather.6 = bf16[1024,256]{1,0:T(8,128)(2,1)S(1)} all-gather(bf16[128,256]{1,0:T(8,128)(2,1)S(1)} %multiply_convert_fusion.1), channel_id=1, replica_groups=mesh['row'=8,'col'=16] {'row'}, dimensions={0}, use_global_device_ids=true | all-gather | bytes 589824 | tf_op jit(solution)/shard_map/all_gather | solution.py:160
  373.5 67.3 %reduce-scatter.17.cloned.1.call-done = bf16[64,256]{1,0:T(8,128)(2,1)} async-done(((bf16[1024,256]{1,0:T(8,128)(2,1)}), bf16[64,256]{1,0:T(8,128)(2,1)}) %reduce-scatter.17.cloned.1.call-update) | async-done | bytes 32784 | tf_op jit(solution)/shard_map/reduce_scatter | solution.py:164
  448.8 7.2 collective-permute-done.16
  463.3 7.5 collective-permute-done.18
  556.5 13.3 %reshape.291 = bf16[128,32768]{1,0:T(8,128)(2,1)} reshape(bf16[8,16,4,64,128]{4,3,2,1,0:T(8,128)(2,1)} %bitcast.249) | data formatting | bytes 16777216 | tf_op jit(solution)/shard_map/reshape | solution.py:170
  575.0 12.4 %all-reduce.1 = f32[1024]{0:T(1024)S(1)} all-reduce(f32[1024]{0:T(1024)S(1)} %get-tuple-element.180), channel_id=8, replica_groups=mesh['row'=8,'col'=16] {'row'}, use_global_device_ids=true, to_apply=%region_12.14.clone | all-reduce | flops 1024 | bytes 8192
  590.0 23.1 %reduce-scatter.21.cloned.1.call-done = f32[128,256]{1,0:T(8,128)} async-done(((f32[1024,256]{1,0:T(8,128)}), f32[128,256]{1,0:T(8,128)}) %reduce-scatter.21.cloned.1.call-update) | async-done | bytes 131088 | tf_op jit(solution)/shard_map/reduce_scatter | solution.py:120
  615.0 33.7 %reduce-scatter.19.cloned.1.call-done = f32[128,512]{1,0:T(8,128)} async-done(((f32[1024,512]{1,0:T(8,128)}), f32[128,512]{1,0:T(8,128)}) %reduce-scatter.19.cloned.1.call-update) | async-done | bytes 262160 | tf_op jit(solution)/shard_map/reduce_scatter | solution.py:118
  657.8 135.6 %while.29 = (s32[]{:T(128)}, f32[8,4,64,128]{3,2,1,0:T(8,128)S(1)}, f32[16,8,4,64]{3,2,1,0:T(4,128)}, bf16[16,8,4,64,128]{4,3,2,0,1:T(8,128)(2,1)}, f32[16,8,4]{...) while((s32[]{:T(128)}, f32[8,4,64,128]{3,2,1,0:T(8,128)S(1)}, ...), condition=%wide.region_16.18_spmd, body=%wide.region_15.17_spmd.sunk | while | flops 4200450 | bytes 3769757 | solution.py:40
  793.4 13.3 %reshape.292 = bf16[128,32768]{1,0:T(8,128)(2,1)} reshape(bf16[8,16,4,64,128]{4,3,2,1,0:T(8,128)(2,1)} %bitcast.247) | data formatting | bytes 16777216 | tf_op jit(solution)/shard_map/reshape | solution.py:170
  821.6 82.0 %psum.15 = f32[128]{0:T(128)S(1)} all-reduce(f32[128]{0:T(128)S(1)} %get-tuple-element.178), channel_id=1, replica_groups=mesh['row'=8,'col'=16] {'col'}, use_global_device_ids=true, to_apply=%region_18.20 | all-reduce | flops 128 | bytes 1024 | tf_op jit(solution)/shard_map/psum | solution.py:152
  903.7 21.5 %all_gather.7 = bf16[1024,256]{1,0:T(8,128)(2,1)S(1)} all-gather(bf16[128,256]{1,0:T(8,128)(2,1)S(1)} %multiply_convert_fusion), channel_id=1, replica_groups=mesh['row'=8,'col'=16] {'row'}, dimensions={0}, use_global_device_ids=true | all-gather | bytes 589824 | tf_op jit(solution)/shard_map/all_gather | solution.py:160
  926.3 13.8 %pad_maximum_fusion = bf16[2,8,16,4,64,128]{5,4,3,2,1,0:T(8,128)(2,1)} fusion(bf16[1,8,16,4,64,128]{5,4,3,2,1,0:T(8,128)(2,1)} %bitcast.248, bf16[1,8,16,4,64,128]{5,4,3,2,1,0:T(8,128)(2,1)} %bitcast.250), kind=kLoop, calls=%fused_computation.22 | loop fusion | flops 8388608 | bytes 33554432 | tf_op jit(solution)/shard_map/stack | solution.py:181
  940.1 55.1 %reduce-scatter.23.cloned.1.call-done = bf16[64,256]{1,0:T(8,128)(2,1)} async-done(((bf16[1024,256]{1,0:T(8,128)(2,1)}), bf16[64,256]{1,0:T(8,128)(2,1)}) %reduce-scatter.23.cloned.1.call-update) | async-done | bytes 32784 | tf_op jit(solution)/shard_map/reduce_scatter | solution.py:164
  (527 shorter events, 417.6 us)
Async XLA Ops:
  7.3 141.2 %reduce-scatter.25.cloned.1.call-start = ((), (), s32[]{:S(2)}) async-start(), calls=%async_computation.15 | async-start | bytes 589824
  7.3 8.5 collective-permute-start
  15.8 7.2 collective-permute-start.1
  23.0 7.2 collective-permute-start.2
  30.3 7.2 collective-permute-start.3
  44.7 7.2 collective-permute-start.5
  52.0 7.2 collective-permute-start.6
  59.2 7.2 collective-permute-start.7
  66.4 7.2 collective-permute-start.8
  73.7 7.2 collective-permute-start.9
  80.9 7.4 collective-permute-start.10
  88.3 7.2 collective-permute-start.11
  95.6 7.2 collective-permute-start.12
  110.0 7.2 collective-permute-start.14
  121.0 61.3 %reduce-scatter.15.cloned.1.call-start = ((), (), s32[]{:S(2)}) async-start(), calls=%async_computation.10 | async-start | bytes 1179648 | tf_op jit(solution)/shard_map/reduce_scatter | solution.py:120
  123.2 94.8 %reduce-scatter.13.cloned.1.call-start = ((), (), s32[]{:S(2)}) async-start(), calls=%async_computation.9 | async-start | bytes 2359296 | tf_op jit(solution)/shard_map/reduce_scatter | solution.py:118
  126.5 314.2 %reduce-scatter.17.cloned.1.call-start = ((), (), s32[]{:S(2)}) async-start(), calls=%async_computation.11 | async-start | bytes 557056 | tf_op jit(solution)/shard_map/reduce_scatter | solution.py:164
  373.4 214.1 %reduce-scatter.27.cloned.1.call-start = ((), (), s32[]{:S(2)}) async-start(), calls=%async_computation.16 | async-start | bytes 589824
  441.5 7.3 collective-permute-start.15
  448.8 7.2 collective-permute-start.16
  463.3 7.5 collective-permute-start.18
  470.8 7.2 collective-permute-start.19
  478.0 7.2 collective-permute-start.20
  485.2 7.2 collective-permute-start.21
  492.5 7.2 collective-permute-start.22
  506.9 7.2 collective-permute-start.24
  514.2 7.2 collective-permute-start.25
  543.1 7.2 collective-permute-start.29
  552.6 60.5 %reduce-scatter.21.cloned.1.call-start = ((), (), s32[]{:S(2)}) async-start(), calls=%async_computation.13 | async-start | bytes 1179648 | tf_op jit(solution)/shard_map/reduce_scatter | solution.py:120
  554.0 94.6 %reduce-scatter.19.cloned.1.call-start = ((), (), s32[]{:S(2)}) async-start(), calls=%async_computation.12 | async-start | bytes 2359296 | tf_op jit(solution)/shard_map/reduce_scatter | solution.py:118
  814.2 182.4 %all-to-all-start = ((bf16[16,2,2,4,64,128]{5,4,3,1,2,0:T(8,128)(2,1)}), bf16[16,2,2,4,64,128]{5,4,3,1,2,0:T(8,128)(2,1)}, u32[]{:S(2)}, u32[]{:S(2)}) async-start(bf16[16,2,2,4,64,128]{5,4,3,1,2,0:T(8,128)(2,1)} %pad_maximum_fusion.1), calls=%async_computation.6 | async-start | bytes 8388608 | tf_op jit(solution)/shard_map/all_to_all | solution.py:177
  821.2 174.1 %reduce-scatter.23.cloned.1.call-start = ((), (), s32[]{:S(2)}) async-start(), calls=%async_computation.14 | async-start | bytes 557056 | tf_op jit(solution)/shard_map/reduce_scatter | solution.py:164
  (35 other events, 3412.0 us)
Sparse Core Ops, SparseCore 0:
  121.1 27.3 reduce-scatter.24
  151.5 30.6 reduce-scatter.14
  185.4 32.5 reduce-scatter.12
  373.5 67.1 reduce-scatter.16
  552.8 27.2 reduce-scatter.26
  582.4 30.6 reduce-scatter.20
  616.2 32.4 reduce-scatter.18
  926.4 68.7 reduce-scatter.22
